TPU v7x, 32 devices: a whole 2x2x4 slice. The times are simulated.
32 devices in a mesh: runs: 2 (over x), sec: 16 (over z, y, core).
Axes of the slice: x: 2, y: 2, z: 4, core: 2. Of those that a mesh axis runs over, the one named last changes fastest.
Arguments:
- edge_rows: bfloat16 [4096, 1024], P(('runs', 'sec')), parts along dimension 0, may hold values from -46 to 46
- corner: bfloat16 [32768, 1024], P(('runs', 'sec')), parts along dimension 0, may hold values from -1 to 2.2
- joining: int32 [32, 16], P('runs'), parts along dimension 0, may hold values from 0 to 15, as said below
- charge_left: int32 [4096], P(('runs', 'sec')), parts along dimension 0, may hold values from 0 to 15
- charge_right: int32 [4096], P(('runs', 'sec')), parts along dimension 0, may hold values from 0 to 15
Outputs:
- isometry: float32 [4096, 1024], P(('runs', 'sec')), parts along dimension 0
There are 2 independent parts, one for each index of `runs`. A program takes and returns all parts, laid end to end along the dimension named above; each array names one. Nothing has to cross between parts.
Inputs may be any that keep to these rules, and one draw needn't show every extreme that they name: joining[charge_left[e], charge_right[e]] names the block that row e needs; each row of joining names every block once; among the 128 rows of one device at most 16 need the same block, and one block, drawn per copy, receives exactly 16 rows from every device.
All inputs are finite; a program needn't handle non-finite values.
Results may differ from a plain program's by a relative error of at most 0.0003.
Values may be sent and summed in bfloat16 or wider, within the bound.
A program may use at most 128 MiB of HBM per device.

v0:
```python
import math
import jax
import jax.numpy as jnp
from jax import lax
from jax.sharding import PartitionSpec as P


def gram_of(images):
    return lax.dot_general(
        images, images, (((0,), (0,)), ((), ())), precision=lax.Precision.HIGHEST
    )


def reduce_gram(partial_gram):
    return lax.psum(partial_gram, "sec")


def solve_rows(gram_total, images, factor):
    lower = jnp.linalg.cholesky(gram_total)
    solved = lax.linalg.triangular_solve(
        lower, images, left_side=False, lower=True, transpose_a=True
    )
    return solved * factor


def per_device(edge_rows, corner, joining, charge_left, charge_right):
    row_count, feature_len = edge_rows.shape
    owners = lax.axis_size("sec")
    capacity = 2 * row_count // owners
    factor = math.sqrt(row_count * owners)
    target = joining[charge_left, charge_right]
    labels = jnp.arange(owners, dtype=jnp.int32)
    onehot = (target[:, None] == labels[None, :]).astype(jnp.int32)
    before = jnp.cumsum(onehot, axis=0) - onehot
    order_in = jnp.sum(before * onehot, axis=1)
    slot_index = target * capacity + order_in
    packed = (
        jnp.zeros((owners * capacity, feature_len), edge_rows.dtype).at[slot_index].set(edge_rows)
    )
    arrived = lax.all_to_all(
        packed.reshape(owners, capacity, feature_len),
        "sec",
        split_axis=0,
        concat_axis=0,
        tiled=True,
    )
    product = jnp.dot(
        arrived.reshape(owners * capacity, feature_len), corner, preferred_element_type=jnp.float32
    )
    returned = lax.all_to_all(
        product.reshape(owners, capacity, feature_len),
        "sec",
        split_axis=0,
        concat_axis=0,
        tiled=True,
    )
    home_rows = returned.reshape(owners * capacity, feature_len)[slot_index]
    gram_total = reduce_gram(gram_of(home_rows))
    result = solve_rows(gram_total, home_rows, factor)
    return result


def solution(mesh):
    placed = (
        P(("runs", "sec"), None),
        P(("runs", "sec"), None),
        P("runs", None),
        P(("runs", "sec")),
        P(("runs", "sec")),
    )
    return jax.shard_map(
        per_device, mesh=mesh, in_specs=placed, out_specs=P(("runs", "sec"), None), check_vma=False
    )
```

profile of v0, /device:TPU:0, one launch (start us, length us, event | category | flops | bytes accessed | tf_op | source)
XLA Modules:
  0.0 532.4 jit_solution(10985662273501543571)
XLA Ops:
  6.5 0.8 fusion.65
  7.4 1.8 gather_fusion
  9.6 1.7 scatter_custom_fusion
  11.4 21.7 %all_to_all.10 = bf16[16,16,1024]{2,1,0:T(8,128)(2,1)S(1)} all-to-all(bf16[16,16,1024]{2,1,0:T(8,128)(2,1)S(1)} %bitcast.114), channel_id=1, replica_groups=mesh['runs'=2,'sec'=16] {'sec'}, dimensions={0} | all-to-all | bytes 1048576 | tf_op jit(solution)/shard_map/all_to_all | solution.py:40
  33.0 1.7 fusion.1
  34.7 4.1 all-to-all-start.1
  38.9 22.9 %all-to-all-done.1 = f32[16,16,1024]{2,1,0:T(8,128)S(1)} async-done(((f32[16,16,1024]{2,1,0:T(8,128)}), f32[16,16,1024]{2,1,0:T(8,128)S(1)}, u32[]{:S(2)}, u32[]{:S(2)}) %all-to-all-start.1) | async-done | bytes 1048608 | tf_op jit(solution)/shard_map/all_to_all | solution.py:50
  61.8 1.6 gather_fusion.1
  63.3 6.6 %fusion.73 = f32[1024,1024]{0,1:T(8,128)} fusion(f32[128,1024]{1,0:T(8,128)} %gather_fusion.1), kind=kOutput, calls=%fused_computation.176 | convolution fusion | flops 1610612736 | bytes 4718592 | tf_op jit(solution)/shard_map/dot_general | solution.py:9
  70.0 113.7 %all-reduce.3.cloned.1.call-done = f32[1024,1024]{0,1:T(8,128)} async-done(((f32[1024,1024]{0,1:T(8,128)}), f32[1024,1024]{0,1:T(8,128)}) %all-reduce.3.cloned.1.call-update) | async-done | bytes 4194320 | tf_op jit(solution)/shard_map/psum | solution.py:15
  183.8 5.8 %copy.10 = f32[1024,1024]{1,0:T(8,128)} copy(f32[1024,1024]{0,1:T(8,128)} %all-reduce.3.cloned.1.call-done) | data formatting | bytes 8388608 | tf_op jit(solution)/shard_map/psum | solution.py:15
  189.6 4.4 fusion
  194.0 1.9 copy-done.1
  195.9 11.7 %cholesky.223 = f32[128,128]{1,0:T(8,128)S(1)} custom-call(f32[128,128]{1,0:T(8,128)S(1)} %cholesky.580), custom_call_target="Cholesky" | custom-call | tf_op jit(solution)/shard_map/jit(cholesky)/cholesky | solution.py:19
  207.7 9.8 %custom-call.62 = f32[1,128,128]{1,2,0:T(8,128)S(1)} custom-call(f32[1,128,128]{2,1,0:T(8,128)S(1)} %get-tuple-element.69), custom_call_target="InvertDiagBlocksLowerTriangular" | custom-call | tf_op jit(solution)/shard_map/jit(cholesky)/cholesky | solution.py:19
  217.5 2.5 cholesky.255
  220.0 2.4 constant_dynamic-update-slice_fusion.31
  222.4 1.5 convolution_subtract_fusion
  223.9 11.9 %cholesky.244 = f32[128,128]{1,0:T(8,128)S(1)} custom-call(f32[128,128]{1,0:T(8,128)S(1)} %cholesky.584), custom_call_target="Cholesky" | custom-call | tf_op jit(solution)/shard_map/jit(cholesky)/cholesky | solution.py:19
  236.4 9.8 %custom-call.63 = f32[1,128,128]{1,2,0:T(8,128)S(1)} custom-call(f32[1,128,128]{2,1,0:T(8,128)S(1)} %get-tuple-element.66), custom_call_target="InvertDiagBlocksLowerTriangular" | custom-call | tf_op jit(solution)/shard_map/jit(cholesky)/cholesky | solution.py:19
  246.3 1.2 convolution_dynamic-update-slice_fusion
  247.5 2.1 convolution_subtract_fusion.1
  249.6 11.7 %cholesky.468 = f32[128,128]{1,0:T(8,128)S(1)} custom-call(f32[128,128]{1,0:T(8,128)S(1)} %cholesky.589), custom_call_target="Cholesky" | custom-call | tf_op jit(solution)/shard_map/jit(cholesky)/cholesky | solution.py:19
  262.0 0.7 compare_reduce_fusion.5
  262.6 9.8 %custom-call.64 = f32[1,128,128]{1,2,0:T(8,128)S(1)} custom-call(f32[1,128,128]{2,1,0:T(8,128)S(1)} %get-tuple-element.63), custom_call_target="InvertDiagBlocksLowerTriangular" | custom-call | tf_op jit(solution)/shard_map/jit(cholesky)/cholesky | solution.py:19
  272.5 1.2 convolution_dynamic-update-slice_fusion.1
  273.6 2.3 convolution_subtract_fusion.2
  276.0 11.9 %cholesky.487 = f32[128,128]{1,0:T(8,128)S(1)} custom-call(f32[128,128]{1,0:T(8,128)S(1)} %cholesky.594), custom_call_target="Cholesky" | custom-call | tf_op jit(solution)/shard_map/jit(cholesky)/cholesky | solution.py:19
  289.2 9.8 %custom-call.65 = f32[1,128,128]{1,2,0:T(8,128)S(1)} custom-call(f32[1,128,128]{2,1,0:T(8,128)S(1)} %get-tuple-element.60), custom_call_target="InvertDiagBlocksLowerTriangular" | custom-call | tf_op jit(solution)/shard_map/jit(cholesky)/cholesky | solution.py:19
  299.0 1.1 convolution_dynamic-update-slice_fusion.2
  300.1 2.3 convolution_subtract_fusion.3
  302.4 11.7 %cholesky.506 = f32[128,128]{1,0:T(8,128)S(1)} custom-call(f32[128,128]{1,0:T(8,128)S(1)} %cholesky.599), custom_call_target="Cholesky" | custom-call | tf_op jit(solution)/shard_map/jit(cholesky)/cholesky | solution.py:19
  315.4 10.2 %custom-call.66 = f32[1,128,128]{1,2,0:T(8,128)S(1)} custom-call(f32[1,128,128]{2,1,0:T(8,128)S(1)} %get-tuple-element.57), custom_call_target="InvertDiagBlocksLowerTriangular" | custom-call | tf_op jit(solution)/shard_map/jit(cholesky)/cholesky | solution.py:19
  325.6 1.0 convolution_dynamic-update-slice_fusion.3
  326.6 2.3 convolution_subtract_fusion.4
  328.9 11.7 %cholesky.526 = f32[128,128]{1,0:T(8,128)S(1)} custom-call(f32[128,128]{1,0:T(8,128)S(1)} %cholesky.604), custom_call_target="Cholesky" | custom-call | tf_op jit(solution)/shard_map/jit(cholesky)/cholesky | solution.py:19
  341.9 9.8 %custom-call.67 = f32[1,128,128]{1,2,0:T(8,128)S(1)} custom-call(f32[1,128,128]{2,1,0:T(8,128)S(1)} %get-tuple-element.54), custom_call_target="InvertDiagBlocksLowerTriangular" | custom-call | tf_op jit(solution)/shard_map/jit(cholesky)/cholesky | solution.py:19
  351.8 0.9 convolution_dynamic-update-slice_fusion.4
  352.7 2.0 convolution_subtract_fusion.5
  354.7 11.9 %cholesky.546 = f32[128,128]{1,0:T(8,128)S(1)} custom-call(f32[128,128]{1,0:T(8,128)S(1)} %cholesky.609), custom_call_target="Cholesky" | custom-call | tf_op jit(solution)/shard_map/jit(cholesky)/cholesky | solution.py:19
  367.9 9.8 %custom-call.68 = f32[1,128,128]{1,2,0:T(8,128)S(1)} custom-call(f32[1,128,128]{2,1,0:T(8,128)S(1)} %get-tuple-element.51), custom_call_target="InvertDiagBlocksLowerTriangular" | custom-call | tf_op jit(solution)/shard_map/jit(cholesky)/cholesky | solution.py:19
  377.7 0.8 convolution_dynamic-update-slice_fusion.6
  378.5 1.8 convolution_subtract_fusion.11
  380.3 11.7 %cholesky.564 = f32[128,128]{1,0:T(8,128)S(1)} custom-call(f32[128,128]{1,0:T(8,128)S(1)} %convolution_subtract_fusion.11), custom_call_target="Cholesky" | custom-call | tf_op jit(solution)/shard_map/jit(cholesky)/cholesky | solution.py:19
  392.6 0.7 compare_reduce_fusion
  398.9 4.8 select_select_fusion
  403.8 27.6 %while.1 = (s32[]{:T(128)}, f32[1024,1024]{1,0:T(8,128)}, s32[8,2]{0,1:T(2,128)S(1)}, f32[8,128,128]{2,1,0:T(8,128)}, s32[]{:T(128)}) while((s32[]{:T(128)}, f32[1024,1024]{1,0:T(8,128)}, s32[8,2]{0,1:T(2,128)S(1)}, f32[8,128,128]{2,1,0:T(8,128)}, s32[]{:T(128)}) %tuple.57), condition=%wide.while_cond, body=%wide.while_body.sunk | while | flops 2 | bytes 132705 | solution.py:20
  404.4 2.9 bitcast_dynamic-update-slice_fusion.2
  407.9 2.8 bitcast_dynamic-update-slice_fusion.2
  411.3 2.8 bitcast_dynamic-update-slice_fusion.2
  414.8 2.8 bitcast_dynamic-update-slice_fusion.2
  418.3 2.8 bitcast_dynamic-update-slice_fusion.2
  421.7 2.8 bitcast_dynamic-update-slice_fusion.2
  425.2 2.8 bitcast_dynamic-update-slice_fusion.2
  428.7 2.8 bitcast_dynamic-update-slice_fusion.2
  431.4 79.6 %custom-call.69 = f32[8,128,128]{1,2,0:T(8,128)S(1)} custom-call(f32[8,128,128]{2,1,0:T(8,128)} %get-tuple-element.12), custom_call_target="InvertDiagBlocksLowerTriangular" | custom-call | tf_op jit(solution)/shard_map/triangular_solve | solution.py:20
  511.4 1.1 convolution_subtract_fusion.10
  512.8 1.3 convolution_subtract_fusion.9
  514.4 1.4 convolution_subtract_fusion.13
  516.1 1.5 convolution_subtract_fusion.12
  518.0 1.7 convolution_subtract_fusion.8
  519.9 1.8 convolution_subtract_fusion.7
  522.0 1.9 convolution_subtract_fusion.6
  524.4 1.0 copy.11
  (60 shorter events, 15.7 us)
Async XLA Ops:
  6.5 26.5 %copy-start = (bf16[1024,1024]{1,0:T(8,128)(2,1)S(1)}, bf16[1024,1024]{1,0:T(8,128)(2,1)}, u32[]{:S(2)}) copy-start(bf16[1024,1024]{1,0:T(8,128)(2,1)} %param.6) | copy-start | bytes 6291460
  34.7 27.0 %all-to-all-start.1 = ((f32[16,16,1024]{2,1,0:T(8,128)}), f32[16,16,1024]{2,1,0:T(8,128)S(1)}, u32[]{:S(2)}, u32[]{:S(2)}) async-start(f32[16,16,1024]{2,1,0:T(8,128)} %fusion.1), calls=%async_computation.1 | async-start | bytes 2097152 | tf_op jit(solution)/shard_map/all_to_all | solution.py:50
  38.8 144.9 %all-reduce.3.cloned.1.call-start = ((), (), s32[]{:S(2)}) async-start(), calls=%async_computation.2 | async-start | bytes 8388608 | tf_op jit(solution)/shard_map/psum | solution.py:15
  194.0 1.9 copy-start.1
  398.9 112.1 %copy-start.2 = (f32[128,1024]{1,0:T(8,128)S(1)}, f32[128,1024]{1,0:T(8,128)}, u32[]{:S(2)}) copy-start(f32[128,1024]{1,0:T(8,128)} %gather_fusion.1) | copy-start | bytes 1572868
Sparse Core Ops, SparseCore 0:
  70.1 113.5 all-reduce.2
where the time goes:
time: 539 us; the launch traced here: 532 us
  other arithmetic  263 us (49%)
  waiting for transfers between devices  137 us (25%)
  matrix products  44.5 us (8%)
  local copies, waits for them, and re-layouts  44 us (8%)
  blocking collectives  21.7 us (4%)
  between operations  18.9 us (4%)
    another operation x30, other arithmetic, solve_rows(): lower = jnp.linalg.cholesky(gram_total)  172 us
    psum x1, waiting for transfers between devices, reduce_gram(): return lax.psum(partial_gram, 'sec')  114 us
    another operation x3, other arithmetic, solve_rows(): lax.linalg.triangular_solve(lower, images, left_side=False, lower=True, t...  84.5 us
    another operation x24, local copies, waits for them, and re-layouts  27.6 us
    another operation x14, matrix products, solve_rows(): lower = jnp.linalg.cholesky(gram_total)  23.1 us
    all_to_all x1, waiting for transfers between devices, per_device(): lax.all_to_all(product.reshape(owners, capacity, feature_len), 'sec', spl...  22.9 us
    all_to_all x1, blocking collectives, per_device(): lax.all_to_all(packed.reshape(owners, capacity, feature_len), 'sec', spli...  21.7 us
    another operation x15, matrix products, solve_rows(): lax.linalg.triangular_solve(lower, images, left_side=False, lower=True, t...  13.1 us
  transfers between devices with their start and end apart: 2, of which 2 were waited for; matrix products, arithmetic and copies ran while one was open for 0% of the time, Pallas kernels for 0%

commit v1 on v0

--- a/solution.py
+++ b/solution.py
@@ -3,6 +3,7 @@
 import jax.numpy as jnp
 from jax import lax
 from jax.sharding import PartitionSpec as P
+from jax.lax import all_gather
 
 
 def gram_of(images):
@@ -12,7 +13,8 @@
 
 
 def reduce_gram(partial_gram):
-    return lax.psum(partial_gram, "sec")
+    group_samples = lambda u_in: jnp.sum(all_gather(u_in, "sec"), axis=0)
+    return group_samples(partial_gram)
 
 
 def solve_rows(gram_total, images, factor):

time: 539 us -> 777 us (1.44)
  waiting for transfers between devices: 137 us -> 351 us
  other arithmetic: 263 us -> 285 us
    all_gather x0 -> x1, waiting for transfers between devices: none -> 328 us  [reduce_gram(): group_samples = lambda u_in: jnp.sum(all_gather(u_in, 'sec'), axis=0)]
    psum x1 -> x0, waiting for transfers between devices: 114 us -> none  [reduce_gram(): return lax.psum(partial_gram, 'sec')]
    reduce_sum x0 -> x1, other arithmetic: none -> 22.9 us  [reduce_gram(): group_samples = lambda u_in: jnp.sum(all_gather(u_in, 'sec'), axis=0)]
where the time goes in v1:
time: 777 us; the launch traced here: 770 us
  waiting for transfers between devices  351 us (45%)
  other arithmetic  285 us (37%)
  matrix products  44.5 us (6%)
  local copies, waits for them, and re-layouts  44 us (6%)
  blocking collectives  21.7 us (3%)
  between operations  18.8 us (2%)
    all_gather x1, waiting for transfers between devices, reduce_gram(): group_samples = lambda u_in: jnp.sum(all_gather(u_in, 'sec'), axis=0)  328 us
    another operation x30, other arithmetic, solve_rows(): lower = jnp.linalg.cholesky(gram_total)  172 us
    another operation x3, other arithmetic, solve_rows(): lax.linalg.triangular_solve(lower, images, left_side=False, lower=True, t...  84.5 us
    another operation x24, local copies, waits for them, and re-layouts  27.6 us
    another operation x14, matrix products, solve_rows(): lower = jnp.linalg.cholesky(gram_total)  23.1 us
    reduce_sum x1, other arithmetic, reduce_gram(): group_samples = lambda u_in: jnp.sum(all_gather(u_in, 'sec'), axis=0)  22.9 us
    all_to_all x1, waiting for transfers between devices, per_device(): lax.all_to_all(product.reshape(owners, capacity, feature_len), 'sec', spl...  22.9 us
    all_to_all x1, blocking collectives, per_device(): lax.all_to_all(packed.reshape(owners, capacity, feature_len), 'sec', spli...  21.7 us
  transfers between devices with their start and end apart: 2, of which 2 were waited for; matrix products, arithmetic and copies ran while one was open for 0% of the time, Pallas kernels for 0%

profile of v1, /device:TPU:0, one launch (start us, length us, event | category | flops | bytes accessed | tf_op | source)
XLA Modules:
  0.0 769.9 jit_solution(12416424832293204199)
XLA Ops:
  6.5 0.8 fusion.65
  7.4 1.8 gather_fusion
  9.6 1.7 scatter_custom_fusion
  11.4 21.7 %all_to_all.10 = bf16[16,16,1024]{2,1,0:T(8,128)(2,1)S(1)} all-to-all(bf16[16,16,1024]{2,1,0:T(8,128)(2,1)S(1)} %bitcast.115), channel_id=1, replica_groups=mesh['runs'=2,'sec'=16] {'sec'}, dimensions={0} | all-to-all | bytes 1048576 | tf_op jit(solution)/shard_map/all_to_all | solution.py:42
  33.0 1.7 fusion.1
  34.7 4.1 all-to-all-start.1
  38.9 22.9 %all-to-all-done.1 = f32[16,16,1024]{2,1,0:T(8,128)S(1)} async-done(((f32[16,16,1024]{2,1,0:T(8,128)}), f32[16,16,1024]{2,1,0:T(8,128)S(1)}, u32[]{:S(2)}, u32[]{:S(2)}) %all-to-all-start.1) | async-done | bytes 1048608 | tf_op jit(solution)/shard_map/all_to_all | solution.py:52
  61.8 1.6 gather_fusion.1
  63.3 6.6 fusion.73
  70.0 328.4 %all-gather.3.cloned.1.call-done = f32[16384,1024]{1,0:T(8,128)} async-done(((f32[1024,1024]{1,0:T(8,128)}), f32[16384,1024]{1,0:T(8,128)}) %all-gather.3.cloned.1.call-update) | async-done | bytes 67108880 | tf_op jit(solution)/shard_map/all_gather | solution.py:16
  398.4 22.9 %reduce_sum.19 = f32[1024,1024]{1,0:T(8,128)} reduce(f32[16,1024,1024]{2,1,0:T(8,128)} %bitcast.5, f32[]{:T(128)} %constant.278.clone.1), dimensions={0}, to_apply=%region_3.4 | reduce | flops 15728640 | bytes 71303168 | tf_op jit(solution)/shard_map/reduce_sum | solution.py:16
  421.4 5.8 copy.10
  427.2 4.4 fusion
  431.6 1.9 copy-done.1
  433.6 11.7 %cholesky.223 = f32[128,128]{1,0:T(8,128)S(1)} custom-call(f32[128,128]{1,0:T(8,128)S(1)} %cholesky.580), custom_call_target="Cholesky" | custom-call | tf_op jit(solution)/shard_map/jit(cholesky)/cholesky | solution.py:21
  445.3 2.5 cholesky.255
  447.8 9.8 %custom-call.62 = f32[1,128,128]{1,2,0:T(8,128)S(1)} custom-call(f32[1,128,128]{2,1,0:T(8,128)S(1)} %get-tuple-element.69), custom_call_target="InvertDiagBlocksLowerTriangular" | custom-call | tf_op jit(solution)/shard_map/jit(cholesky)/cholesky | solution.py:21
  457.6 2.4 constant_dynamic-update-slice_fusion.31
  460.0 1.5 convolution_subtract_fusion
  461.6 11.9 %cholesky.244 = f32[128,128]{1,0:T(8,128)S(1)} custom-call(f32[128,128]{1,0:T(8,128)S(1)} %cholesky.584), custom_call_target="Cholesky" | custom-call | tf_op jit(solution)/shard_map/jit(cholesky)/cholesky | solution.py:21
  474.1 9.8 %custom-call.63 = f32[1,128,128]{1,2,0:T(8,128)S(1)} custom-call(f32[1,128,128]{2,1,0:T(8,128)S(1)} %get-tuple-element.66), custom_call_target="InvertDiagBlocksLowerTriangular" | custom-call | tf_op jit(solution)/shard_map/jit(cholesky)/cholesky | solution.py:21
  483.9 1.2 convolution_dynamic-update-slice_fusion
  485.1 2.1 convolution_subtract_fusion.1
  487.2 11.7 %cholesky.468 = f32[128,128]{1,0:T(8,128)S(1)} custom-call(f32[128,128]{1,0:T(8,128)S(1)} %cholesky.589), custom_call_target="Cholesky" | custom-call | tf_op jit(solution)/shard_map/jit(cholesky)/cholesky | solution.py:21
  500.2 9.8 %custom-call.64 = f32[1,128,128]{1,2,0:T(8,128)S(1)} custom-call(f32[1,128,128]{2,1,0:T(8,128)S(1)} %get-tuple-element.63), custom_call_target="InvertDiagBlocksLowerTriangular" | custom-call | tf_op jit(solution)/shard_map/jit(cholesky)/cholesky | solution.py:21
  510.0 1.2 convolution_dynamic-update-slice_fusion.1
  511.2 2.3 convolution_subtract_fusion.2
  513.5 11.9 %cholesky.487 = f32[128,128]{1,0:T(8,128)S(1)} custom-call(f32[128,128]{1,0:T(8,128)S(1)} %cholesky.594), custom_call_target="Cholesky" | custom-call | tf_op jit(solution)/shard_map/jit(cholesky)/cholesky | solution.py:21
  526.7 9.8 %custom-call.65 = f32[1,128,128]{1,2,0:T(8,128)S(1)} custom-call(f32[1,128,128]{2,1,0:T(8,128)S(1)} %get-tuple-element.60), custom_call_target="InvertDiagBlocksLowerTriangular" | custom-call | tf_op jit(solution)/shard_map/jit(cholesky)/cholesky | solution.py:21
  536.5 1.1 convolution_dynamic-update-slice_fusion.2
  537.6 2.3 convolution_subtract_fusion.3
  540.0 11.7 %cholesky.506 = f32[128,128]{1,0:T(8,128)S(1)} custom-call(f32[128,128]{1,0:T(8,128)S(1)} %cholesky.599), custom_call_target="Cholesky" | custom-call | tf_op jit(solution)/shard_map/jit(cholesky)/cholesky | solution.py:21
  553.0 10.2 %custom-call.66 = f32[1,128,128]{1,2,0:T(8,128)S(1)} custom-call(f32[1,128,128]{2,1,0:T(8,128)S(1)} %get-tuple-element.57), custom_call_target="InvertDiagBlocksLowerTriangular" | custom-call | tf_op jit(solution)/shard_map/jit(cholesky)/cholesky | solution.py:21
  563.2 1.0 convolution_dynamic-update-slice_fusion.3
  564.2 2.3 convolution_subtract_fusion.4
  566.5 11.7 %cholesky.526 = f32[128,128]{1,0:T(8,128)S(1)} custom-call(f32[128,128]{1,0:T(8,128)S(1)} %cholesky.604), custom_call_target="Cholesky" | custom-call | tf_op jit(solution)/shard_map/jit(cholesky)/cholesky | solution.py:21
  579.5 9.8 %custom-call.67 = f32[1,128,128]{1,2,0:T(8,128)S(1)} custom-call(f32[1,128,128]{2,1,0:T(8,128)S(1)} %get-tuple-element.54), custom_call_target="InvertDiagBlocksLowerTriangular" | custom-call | tf_op jit(solution)/shard_map/jit(cholesky)/cholesky | solution.py:21
  589.3 0.9 convolution_dynamic-update-slice_fusion.4
  590.2 2.0 convolution_subtract_fusion.5
  592.3 11.9 %cholesky.546 = f32[128,128]{1,0:T(8,128)S(1)} custom-call(f32[128,128]{1,0:T(8,128)S(1)} %cholesky.609), custom_call_target="Cholesky" | custom-call | tf_op jit(solution)/shard_map/jit(cholesky)/cholesky | solution.py:21
  605.4 9.8 %custom-call.68 = f32[1,128,128]{1,2,0:T(8,128)S(1)} custom-call(f32[1,128,128]{2,1,0:T(8,128)S(1)} %get-tuple-element.51), custom_call_target="InvertDiagBlocksLowerTriangular" | custom-call | tf_op jit(solution)/shard_map/jit(cholesky)/cholesky | solution.py:21
  615.2 0.8 convolution_dynamic-update-slice_fusion.6
  616.0 1.8 convolution_subtract_fusion.11
  617.8 11.7 %cholesky.564 = f32[128,128]{1,0:T(8,128)S(1)} custom-call(f32[128,128]{1,0:T(8,128)S(1)} %convolution_subtract_fusion.11), custom_call_target="Cholesky" | custom-call | tf_op jit(solution)/shard_map/jit(cholesky)/cholesky | solution.py:21
  630.2 0.7 compare_reduce_fusion
  636.4 4.8 select_select_fusion
  641.2 27.7 %while.1 = (s32[]{:T(128)}, f32[1024,1024]{1,0:T(8,128)}, s32[8,2]{0,1:T(2,128)S(1)}, f32[8,128,128]{2,1,0:T(8,128)}, s32[]{:T(128)}) while((s32[]{:T(128)}, f32[1024,1024]{1,0:T(8,128)}, s32[8,2]{0,1:T(2,128)S(1)}, f32[8,128,128]{2,1,0:T(8,128)}, s32[]{:T(128)}) %tuple.57), condition=%wide.while_cond, body=%wide.while_body.sunk | while | flops 2 | bytes 132705 | solution.py:22
  641.9 2.8 bitcast_dynamic-update-slice_fusion.2
  645.3 2.8 bitcast_dynamic-update-slice_fusion.2
  648.8 2.8 bitcast_dynamic-update-slice_fusion.2
  652.2 2.8 bitcast_dynamic-update-slice_fusion.2
  655.7 2.8 bitcast_dynamic-update-slice_fusion.2
  659.2 2.9 bitcast_dynamic-update-slice_fusion.2
  662.7 2.8 bitcast_dynamic-update-slice_fusion.2
  666.1 2.8 bitcast_dynamic-update-slice_fusion.2
  668.9 79.6 %custom-call.69 = f32[8,128,128]{1,2,0:T(8,128)S(1)} custom-call(f32[8,128,128]{2,1,0:T(8,128)} %get-tuple-element.12), custom_call_target="InvertDiagBlocksLowerTriangular" | custom-call | tf_op jit(solution)/shard_map/triangular_solve | solution.py:22
  748.8 1.1 convolution_subtract_fusion.10
  750.2 1.3 convolution_subtract_fusion.9
  751.8 1.4 convolution_subtract_fusion.13
  753.6 1.5 convolution_subtract_fusion.12
  755.4 1.7 convolution_subtract_fusion.8
  757.4 1.8 convolution_subtract_fusion.7
  759.5 1.9 convolution_subtract_fusion.6
  761.8 1.0 copy.11
  (61 shorter events, 16.2 us)
Async XLA Ops:
  6.5 26.5 %copy-start = (bf16[1024,1024]{1,0:T(8,128)(2,1)S(1)}, bf16[1024,1024]{1,0:T(8,128)(2,1)}, u32[]{:S(2)}) copy-start(bf16[1024,1024]{1,0:T(8,128)(2,1)} %param.6) | copy-start | bytes 6291460
  34.7 27.0 %all-to-all-start.1 = ((f32[16,16,1024]{2,1,0:T(8,128)}), f32[16,16,1024]{2,1,0:T(8,128)S(1)}, u32[]{:S(2)}, u32[]{:S(2)}) async-start(f32[16,16,1024]{2,1,0:T(8,128)} %fusion.1), calls=%async_computation.1 | async-start | bytes 2097152 | tf_op jit(solution)/shard_map/all_to_all | solution.py:52
  38.8 359.6 %all-gather.3.cloned.1.call-start = ((), (), s32[]{:S(2)}) async-start(), calls=%async_computation.2 | async-start | bytes 71303168 | tf_op jit(solution)/shard_map/all_gather | solution.py:16
  431.6 1.9 copy-start.1
  636.4 112.1 %copy-start.2 = (f32[128,1024]{1,0:T(8,128)S(1)}, f32[128,1024]{1,0:T(8,128)}, u32[]{:S(2)}) copy-start(f32[128,1024]{1,0:T(8,128)} %gather_fusion.1) | copy-start | bytes 1572868
Sparse Core Ops, SparseCore 0:
  70.1 328.2 all-gather.2
